TPU v7x, 256 devices: a whole 4x4x8 slice. The times are simulated.
256 devices in a mesh: dp: 4 (over z_lo), space: 64 (over z_hi, x, y, core).
Axes of the slice: x: 4, y: 4, z: 8 (z_hi: 2, z_lo: 4; z = z_hi * 4 + z_lo), core: 2. Of those that a mesh axis runs over, the one named last changes fastest.
Arguments:
- volumes: bfloat16 [4, 64, 2, 8, 16, 256], P('dp', 'space'), may hold values from -6 to 6
- weight: bfloat16 [256, 6912], P('space', 'dp'), may hold values from -0.078125 to 0.078125
- cotangent: bfloat16 [4, 64, 2, 8, 16, 256], P('dp', 'space'), may hold values from -6 to 6
Outputs:
- features: bfloat16 [4, 64, 2, 8, 16, 256], P('dp', 'space')
- input_grad: bfloat16 [4, 64, 2, 8, 16, 256], P('dp', 'space')
- weight_grad: float32 [256, 6912], P('space', 'dp')
All inputs are finite; a program needn't handle non-finite values.
Results may differ from a plain program's by a relative error of at most 0.0034.
Values may be sent and summed in bfloat16 or wider, within the bound.
No kernel may reach another device: no remote copies, remote signals or barrier semaphores. Data moves between devices by JAX's collectives and lax.ppermute only.
A program may use at most 128 MiB of HBM per device.

v0:
```python
import math
import jax
import jax.numpy as jnp
from jax import lax
from jax.sharding import PartitionSpec as P


def from_behind(block, axis, distance):
    devices = range(lax.axis_size(axis))
    route = [((i - distance) % len(devices), i) for i in devices]
    return lax.ppermute(block, axis, route)


def tap_view(padded, tap, flipped):
    first = tap // 9
    second = tap // 3 % 3
    third = tap % 3
    if flipped:
        first, second, third = (2 - first, 2 - second, 2 - third)
    vols, depth, height, width, chans = padded.shape
    view = padded[
        :, first : first + depth - 2, second : second + height - 2, third : third + width - 2, :
    ]
    return view.reshape(-1, chans)


def per_device(volumes, weight, cotangent):
    own_in = volumes[:, 0]
    own_cot = cotangent[:, 0]
    chans = own_in.shape[-1]
    blocks = lax.axis_size("space")
    grid_cols = min(8, blocks // 2)
    stacked = jnp.stack((own_in, own_cot))
    from_lower = from_behind(stacked[:, :, -1:], "space", grid_cols)
    from_upper = from_behind(stacked[:, :, :1], "space", -grid_cols)
    ext_x = jnp.concatenate((from_lower, stacked, from_upper), axis=2)
    side_lower = from_behind(ext_x[:, :, :, -1:], "space", 1)
    side_upper = from_behind(ext_x[:, :, :, :1], "space", -1)
    ext_xy = jnp.concatenate((side_lower, ext_x, side_upper), axis=3)
    padded = jnp.pad(ext_xy, ((0, 0), (0, 0), (0, 0), (0, 0), (1, 1), (0, 0)))
    in_pad = padded[0]
    cot_pad = padded[1]
    wide = lax.all_gather(weight, "dp", axis=1, tiled=True)
    full_weight = lax.all_gather(wide, "space", axis=0, tiled=True)
    cot_flat = own_cot.reshape(-1, chans)
    cells = cot_flat.shape[0]
    output = jnp.zeros((cells, chans), jnp.float32)
    grad_in = jnp.zeros((cells, chans), jnp.float32)
    grad_blocks = []
    for tap in range(27):
        kernel_tap = full_weight[:, tap * chans : (tap + 1) * chans]
        in_view = tap_view(in_pad, tap, False)
        output = output + lax.dot_general(
            in_view, kernel_tap, (((1,), (1,)), ((), ())), preferred_element_type=jnp.float32
        )
        grad_in = grad_in + jnp.dot(
            tap_view(cot_pad, tap, True), kernel_tap, preferred_element_type=jnp.float32
        )
        grad_blocks.append(
            lax.dot_general(
                cot_flat, in_view, (((0,), (0,)), ((), ())), preferred_element_type=jnp.float32
            )
        )
    features = output.astype(jnp.bfloat16).reshape(volumes.shape)
    input_grad = grad_in.astype(jnp.bfloat16).reshape(volumes.shape)
    voxel_count = cells * lax.axis_size("dp") * blocks
    factor = 1.0 / math.sqrt(voxel_count)
    local_grad = jnp.concatenate(grad_blocks, axis=1) * factor
    partial_rows = lax.psum_scatter(local_grad, "space", scatter_dimension=0, tiled=True)
    weight_grad = lax.psum_scatter(partial_rows, "dp", scatter_dimension=1, tiled=True)
    return (features, input_grad, weight_grad)


def solution(mesh):
    return jax.shard_map(
        per_device,
        mesh=mesh,
        in_specs=(
            P("dp", "space", None, None, None, None),
            P("space", "dp"),
            P("dp", "space", None, None, None, None),
        ),
        out_specs=(
            P("dp", "space", None, None, None, None),
            P("dp", "space", None, None, None, None),
            P("space", "dp"),
        ),
        check_vma=False,
    )
```

profile of v0, /device:TPU:1, one launch (start us, length us, event | category | flops | bytes accessed | tf_op | source)
XLA Modules:
  0.0 1021.1 jit_solution(11820296682975648662)
XLA Ops:
  7.2 0.9 constant_dynamic-update-slice_fusion.1
  8.1 0.9 constant_dynamic-update-slice_fusion
  9.1 10.0 collective-permute-start.1
  19.1 4.8 collective-permute-done.1
  23.9 8.3 collective-permute-done
  32.2 1.7 collective-permute-start.3
  33.9 1.3 collective-permute-start.2
  35.1 11.0 %all-gather = bf16[4,1728,4]{1,2,0:T(4,128)(2,1)S(1)} all-gather(bf16[1,1728,4]{1,2,0:T(4,128)(2,1)} %bitcast.399), channel_id=1, replica_groups=mesh['dp'=4,'space'=64] {'dp'}, dimensions={0}, use_global_device_ids=true | all-gather | bytes 69120 | tf_op jit(solution)/shard_map/all_gather | solution.py:43
  46.2 0.7 reshape.231
  47.0 1.3 dynamic-slice
  48.9 0.6 select_maximum_fusion
  49.6 0.3 fusion.93
  50.1 1.5 fusion.92
  57.8 0.2 fusion.1
  58.0 1.5 fusion.91
  59.6 3.4 broadcast_multiply_fusion
  63.2 72.8 %all-gather.4.cloned.1.call-done = bf16[64,4,6912]{2,1,0:T(4,128)(2,1)} async-done(((bf16[1,4,6912]{2,1,0:T(4,128)(2,1)}), bf16[64,4,6912]{2,1,0:T(4,128)(2,1)}) %all-gather.4.cloned.1.call-update) | async-done | bytes 3538960 | tf_op jit(solution)/shard_map/all_gather | solution.py:44
  136.0 5.3 reshape.233
  141.4 1.2 fusion.89
  142.6 1.2 convolution_add_fusion.51
  143.7 1.2 convolution_add_fusion.50
  144.9 1.2 convolution_add_fusion.49
  146.1 1.2 convolution_add_fusion.48
  147.8 0.2 convolution_add_fusion.45
  149.8 0.2 convolution_add_fusion.37
  152.7 0.9 fusion.28
  158.7 0.9 convolution_add_fusion.1
  159.6 775.8 %all-reduce.4.cloned.1.call-done = f32[256,6912]{0,1:T(8,128)} async-done(((f32[256,6912]{0,1:T(8,128)}), f32[256,6912]{0,1:T(8,128)}) %all-reduce.4.cloned.1.call-update) | async-done | bytes 7077904
  935.4 4.8 constant_dynamic-slice_fusion
  940.2 1.9 fusion.29
  942.0 70.4 %reduce-scatter.3.cloned.1.call-done = f32[4,1728]{0,1:T(8,128)} async-done(((f32[4,6912]{0,1:T(8,128)}), f32[4,1728]{0,1:T(8,128)}) %reduce-scatter.3.cloned.1.call-update) | async-done | bytes 27664 | tf_op jit(solution)/shard_map/reduce_scatter | solution.py:70
  1012.5 2.1 copy.10
  (235 shorter events, 15.4 us)
Async XLA Ops:
  7.2 128.8 %all-gather.4.cloned.1.call-start = ((), (), s32[]{:S(2)}) async-start(), calls=%async_computation.2 | async-start | bytes 3594240 | tf_op jit(solution)/shard_map/all_gather | solution.py:44
  9.1 14.8 %collective-permute-start.1 = (bf16[2,1,1,8,16,256]{5,4,3,2,1,0:T(8,128)(2,1)S(1)}, bf16[2,1,1,8,16,256]{5,4,3,2,1,0:T(8,128)(2,1)S(1)}, u32[]{:S(2)}, u32[]{:S(2)}) collective-permute-start(bf16[2,1,1,8,16,256]{5,4,3,2,1,0:T(8,128)(2,1)S(1)} %get-tuple-element.71), channel_id=1, source_target_pairs={{8,0},{9,1},{10,2},{11,3},{12,4},{13,5},{14,6},{15,7},{16,8},{17,9... | collective-permute-start | bytes 393224 | tf_op jit(solution)/shard_map/ppermute | solution.py:11
  19.1 13.1 %collective-permute-start = (bf16[2,1,1,8,16,256]{5,4,3,2,1,0:T(8,128)(2,1)S(1)}, bf16[2,1,1,8,16,256]{5,4,3,2,1,0:T(8,128)(2,1)S(1)}, u32[]{:S(2)}, u32[]{:S(2)}) collective-permute-start(bf16[2,1,1,8,16,256]{5,4,3,2,1,0:T(8,128)(2,1)S(1)} %get-tuple-element.70), channel_id=1, source_target_pairs={{56,0},{57,1},{58,2},{59,3},{60,4},{61,5},{62,6},{63,7},{0,8},{1,9... | collective-permute-start | bytes 393224 | tf_op jit(solution)/shard_map/ppermute | solution.py:11
  32.2 16.7 %collective-permute-start.3 = (bf16[2,1,4,1,16,256]{5,4,3,2,1,0:T(8,128)(2,1)S(1)}, bf16[2,1,4,1,16,256]{5,4,3,2,1,0:T(8,128)(2,1)S(1)}, u32[]{:S(2)}, u32[]{:S(2)}) collective-permute-start(bf16[2,1,4,1,16,256]{5,4,3,2,1,0:T(8,128)(2,1)S(1)} %get-tuple-element.15), channel_id=1, source_target_pairs={{1,0},{2,1},{3,2},{4,3},{5,4},{6,5},{7,6},{8,7},{9,8},{10,9},{11,1... | collective-permute-start | bytes 196616 | tf_op jit(solution)/shard_map/ppermute | solution.py:11
  33.9 15.1 %collective-permute-start.2 = (bf16[2,1,4,1,16,256]{5,4,3,2,1,0:T(8,128)(2,1)S(1)}, bf16[2,1,4,1,16,256]{5,4,3,2,1,0:T(8,128)(2,1)S(1)}, u32[]{:S(2)}, u32[]{:S(2)}) collective-permute-start(bf16[2,1,4,1,16,256]{5,4,3,2,1,0:T(8,128)(2,1)S(1)} %get-tuple-element.14), channel_id=1, source_target_pairs={{63,0},{0,1},{1,2},{2,3},{3,4},{4,5},{5,6},{6,7},{7,8},{8,9},{9,10... | collective-permute-start | bytes 196616 | tf_op jit(solution)/shard_map/ppermute | solution.py:11
  46.9 888.4 %all-reduce.4.cloned.1.call-start = ((), (), s32[]{:S(2)}) async-start(), calls=%async_computation.3 | async-start | bytes 14155776
  49.9 4.1 copy-start.33
  49.9 4.3 copy-start.31
  49.9 4.5 copy-start.29
  49.9 4.7 copy-start.27
  49.9 5.0 copy-start.25
  50.0 5.3 copy-start.23
  50.0 5.5 copy-start.21
  50.0 5.7 copy-start.19
  50.0 5.9 copy-start.17
  50.0 6.2 copy-start.15
  50.0 6.4 copy-start.13
  50.0 6.6 copy-start.11
  50.0 6.8 copy-start.9
  50.0 7.1 copy-start.7
  50.0 7.3 copy-start.5
  50.1 7.5 copy-start.3
  50.1 7.8 copy-start.1
  63.0 949.5 %reduce-scatter.3.cloned.1.call-start = ((), (), s32[]{:S(2)}) async-start(), calls=%async_computation.1 | async-start | bytes 4423680 | tf_op jit(solution)/shard_map/reduce_scatter | solution.py:70
  141.3 6.0 copy-start.44
  141.3 6.2 copy-start.42
  141.3 6.4 copy-start.40
  141.3 6.7 copy-start.38
  141.4 6.9 copy-start.36
  142.6 6.0 copy-start.34
  143.7 5.0 copy-start.32
  144.9 4.1 copy-start.30
  (51 other events, 125.2 us)
Sparse Core Ops, SparseCore 0:
  47.0 88.9 all-gather.3
  138.7 796.6 all-reduce.3
  940.3 72.1 reduce-scatter.2
where the time goes:
time: 1020 us
  waiting for transfers between devices  932 us (91%)
  matrix products  24.7 us (2%)
  local copies, waits for them, and re-layouts  19.8 us (2%)
  between operations  16.2 us (2%)
  starting transfers between devices  13.3 us (1%)
  blocking collectives  11 us (1%)
    unnamed x4, waiting for transfers between devices  776 us
    all_gather x1, waiting for transfers between devices, per_device(): full_weight = lax.all_gather(wide, 'space', axis=0, tiled=True)  72.8 us
    reduce_scatter x1, waiting for transfers between devices, per_device(): lax.psum_scatter(partial_rows, 'dp', scatter_dimension=1, tiled=True)  70.4 us
  transfers between devices with their start and end apart: 7, of which 5 were waited for; matrix products, arithmetic and copies ran while one was open for 4% of the time, Pallas kernels for 0%

commit v1 on v0

--- a/solution.py
+++ b/solution.py
@@ -3,6 +3,19 @@
 import jax.numpy as jnp
 from jax import lax
 from jax.sharding import PartitionSpec as P
+
+
+def post_columns(x_part, shard_axis):
+    k_now = jnp.concatenate(
+        jax.lax.all_to_all(
+            jnp.stack(jax.lax.axis_size(shard_axis) * [x_part]),
+            axis_name=shard_axis,
+            split_axis=0,
+            concat_axis=0,
+        ),
+        axis=0,
+    )
+    return k_now
 
 
 def from_behind(block, axis, distance):
@@ -41,7 +54,7 @@
     in_pad = padded[0]
     cot_pad = padded[1]
     wide = lax.all_gather(weight, "dp", axis=1, tiled=True)
-    full_weight = lax.all_gather(wide, "space", axis=0, tiled=True)
+    full_weight = post_columns(wide, "space")
     cot_flat = own_cot.reshape(-1, chans)
     cells = cot_flat.shape[0]
     output = jnp.zeros((cells, chans), jnp.float32)

time: 1020 us -> 980 us (0.961)
  waiting for transfers between devices: 932 us -> 878 us
  starting transfers between devices: 13.3 us -> 24.7 us
    all_gather x1 -> x0, waiting for transfers between devices: 72.8 us -> none  [per_device(): full_weight = lax.all_gather(wide, 'space', axis=0, tiled=True)]
    all_to_all x0 -> x1, waiting for transfers between devices: none -> 71.3 us  [post_columns(): jax.lax.all_to_all(jnp.stack(jax.lax.axis_size(shard_axis) * [x_part]), a...]
    unnamed x4 -> x3, waiting for transfers between devices: 776 us -> 723 us
    all_to_all x0 -> x1, starting transfers between devices: none -> 11.5 us  [post_columns(): jax.lax.all_to_all(jnp.stack(jax.lax.axis_size(shard_axis) * [x_part]), a...]
where the time goes in v1:
time: 980 us
  waiting for transfers between devices  878 us (90%)
  starting transfers between devices  24.7 us (3%)
  matrix products  24.7 us (3%)
  local copies, waits for them, and re-layouts  21.2 us (2%)
  between operations  16.5 us (2%)
  blocking collectives  11 us (1%)
    unnamed x3, waiting for transfers between devices  723 us
    all_to_all x1, waiting for transfers between devices, post_columns(): jax.lax.all_to_all(jnp.stack(jax.lax.axis_size(shard_axis) * [x_part]), a...  71.3 us
    reduce_scatter x1, waiting for transfers between devices, per_device(): lax.psum_scatter(partial_rows, 'dp', scatter_dimension=1, tiled=True)  70.4 us
  transfers between devices with their start and end apart: 7, of which 5 were waited for; matrix products, arithmetic and copies ran while one was open for 4% of the time, Pallas kernels for 0%

profile of v1, /device:TPU:1, one launch (start us, length us, event | category | flops | bytes accessed | tf_op | source)
XLA Modules:
  0.0 979.7 jit_solution(9610871365969354187)
XLA Ops:
  7.2 0.9 constant_dynamic-update-slice_fusion.1
  8.1 0.9 constant_dynamic-update-slice_fusion
  9.0 10.0 %collective-permute-start.1 = (bf16[2,1,1,8,16,256]{5,4,3,2,1,0:T(8,128)(2,1)S(1)}, bf16[2,1,1,8,16,256]{5,4,3,2,1,0:T(8,128)(2,1)S(1)}, u32[]{:S(2)}, u32[]{:S(2)}) collective-permute-start(bf16[2,1,1,8,16,256]{5,4,3,2,1,0:T(8,128)(2,1)S(1)} %get-tuple-element.71), channel_id=1, source_target_pairs={{8,0},{9,1},{10,2},{11,3},{12,4},{13,5},{14,6},{15,7},{16,8},{17,9... | collective-permute-start | bytes 393224 | tf_op jit(solution)/shard_map/ppermute | solution.py:24
  19.0 4.8 collective-permute-done.1
  23.8 8.3 collective-permute-done
  32.1 1.7 collective-permute-start.3
  33.8 1.3 collective-permute-start.2
  35.1 11.0 %all-gather = bf16[4,1728,4]{1,2,0:T(4,128)(2,1)S(1)} all-gather(bf16[1,1728,4]{1,2,0:T(4,128)(2,1)} %bitcast.397), channel_id=1, replica_groups=mesh['dp'=4,'space'=64] {'dp'}, dimensions={0}, use_global_device_ids=true | all-gather | bytes 69120 | tf_op jit(solution)/shard_map/all_gather | solution.py:56
  46.2 2.7 stack.5
  48.9 11.5 %all-to-all-start = ((bf16[64,4,6912]{2,1,0:T(4,128)(2,1)}), bf16[64,4,6912]{2,1,0:T(4,128)(2,1)}, u32[]{:S(2)}, u32[]{:S(2)}) async-start(bf16[64,4,6912]{2,1,0:T(4,128)(2,1)} %stack.5), calls=%async_computation | async-start | bytes 7077888 | tf_op jit(solution)/shard_map/all_to_all | solution.py:10
  60.5 0.6 dynamic-slice
  61.7 0.6 select_maximum_fusion
  62.4 0.3 fusion.93
  62.9 1.5 fusion.92
  70.8 3.4 broadcast_multiply_fusion
  74.5 1.5 fusion.91
  76.0 71.3 %all-to-all-done = bf16[64,4,6912]{2,1,0:T(4,128)(2,1)} async-done(((bf16[64,4,6912]{2,1,0:T(4,128)(2,1)}), bf16[64,4,6912]{2,1,0:T(4,128)(2,1)}, u32[]{:S(2)}, u32[]{:S(2)}) %all-to-all-start) | async-done | bytes 3538976 | tf_op jit(solution)/shard_map/all_to_all | solution.py:10
  147.3 5.3 reshape.180
  152.7 1.2 fusion.89
  153.9 1.2 convolution_add_fusion.51
  155.1 1.2 convolution_add_fusion.50
  156.3 1.2 convolution_add_fusion.49
  157.5 1.2 convolution_add_fusion.48
  161.1 0.2 convolution_add_fusion.37
  163.3 0.2 convolution_add_fusion.29
  164.1 0.9 fusion.28
  170.0 0.9 convolution_add_fusion.1
  170.9 722.7 %all-reduce.4.cloned.1.call-done = f32[256,6912]{0,1:T(8,128)} async-done(((f32[256,6912]{0,1:T(8,128)}), f32[256,6912]{0,1:T(8,128)}) %all-reduce.4.cloned.1.call-update) | async-done | bytes 7077904
  893.6 4.8 constant_dynamic-slice_fusion
  898.4 1.9 fusion.29
  900.3 70.4 %reduce-scatter.3.cloned.1.call-done = f32[4,1728]{0,1:T(8,128)} async-done(((f32[4,6912]{0,1:T(8,128)}), f32[4,1728]{0,1:T(8,128)}) %reduce-scatter.3.cloned.1.call-update) | async-done | bytes 27664 | tf_op jit(solution)/shard_map/reduce_scatter | solution.py:83
  970.8 2.1 copy.11
  (237 shorter events, 15.7 us)
Async XLA Ops:
  9.0 14.8 %collective-permute-start.1 = (bf16[2,1,1,8,16,256]{5,4,3,2,1,0:T(8,128)(2,1)S(1)}, bf16[2,1,1,8,16,256]{5,4,3,2,1,0:T(8,128)(2,1)S(1)}, u32[]{:S(2)}, u32[]{:S(2)}) collective-permute-start(bf16[2,1,1,8,16,256]{5,4,3,2,1,0:T(8,128)(2,1)S(1)} %get-tuple-element.71), channel_id=1, source_target_pairs={{8,0},{9,1},{10,2},{11,3},{12,4},{13,5},{14,6},{15,7},{16,8},{17,9... | collective-permute-start | bytes 393224 | tf_op jit(solution)/shard_map/ppermute | solution.py:24
  19.0 13.1 %collective-permute-start = (bf16[2,1,1,8,16,256]{5,4,3,2,1,0:T(8,128)(2,1)S(1)}, bf16[2,1,1,8,16,256]{5,4,3,2,1,0:T(8,128)(2,1)S(1)}, u32[]{:S(2)}, u32[]{:S(2)}) collective-permute-start(bf16[2,1,1,8,16,256]{5,4,3,2,1,0:T(8,128)(2,1)S(1)} %get-tuple-element.70), channel_id=1, source_target_pairs={{56,0},{57,1},{58,2},{59,3},{60,4},{61,5},{62,6},{63,7},{0,8},{1,9... | collective-permute-start | bytes 393224 | tf_op jit(solution)/shard_map/ppermute | solution.py:24
  32.1 29.6 %collective-permute-start.3 = (bf16[2,1,4,1,16,256]{5,4,3,2,1,0:T(8,128)(2,1)S(1)}, bf16[2,1,4,1,16,256]{5,4,3,2,1,0:T(8,128)(2,1)S(1)}, u32[]{:S(2)}, u32[]{:S(2)}) collective-permute-start(bf16[2,1,4,1,16,256]{5,4,3,2,1,0:T(8,128)(2,1)S(1)} %get-tuple-element.15), channel_id=1, source_target_pairs={{1,0},{2,1},{3,2},{4,3},{5,4},{6,5},{7,6},{8,7},{9,8},{10,9},{11,1... | collective-permute-start | bytes 196616 | tf_op jit(solution)/shard_map/ppermute | solution.py:24
  33.8 27.9 %collective-permute-start.2 = (bf16[2,1,4,1,16,256]{5,4,3,2,1,0:T(8,128)(2,1)S(1)}, bf16[2,1,4,1,16,256]{5,4,3,2,1,0:T(8,128)(2,1)S(1)}, u32[]{:S(2)}, u32[]{:S(2)}) collective-permute-start(bf16[2,1,4,1,16,256]{5,4,3,2,1,0:T(8,128)(2,1)S(1)} %get-tuple-element.14), channel_id=1, source_target_pairs={{63,0},{0,1},{1,2},{2,3},{3,4},{4,5},{5,6},{6,7},{7,8},{8,9},{9,10... | collective-permute-start | bytes 196616 | tf_op jit(solution)/shard_map/ppermute | solution.py:24
  48.9 11.5 %copy-start.76 = (u32[256]{0:T(256)S(1)}, u32[256]{0:T(256)}, u32[]{:S(2)}) copy-start(u32[256]{0:T(256)} %constant.12) | copy-start | bytes 3076
  48.9 98.4 %all-to-all-start = ((bf16[64,4,6912]{2,1,0:T(4,128)(2,1)}), bf16[64,4,6912]{2,1,0:T(4,128)(2,1)}, u32[]{:S(2)}, u32[]{:S(2)}) async-start(bf16[64,4,6912]{2,1,0:T(4,128)(2,1)} %stack.5), calls=%async_computation | async-start | bytes 7077888 | tf_op jit(solution)/shard_map/all_to_all | solution.py:10
  60.4 833.2 %all-reduce.4.cloned.1.call-start = ((), (), s32[]{:S(2)}) async-start(), calls=%async_computation.3 | async-start | bytes 14155776
  62.7 4.2 copy-start.31
  62.7 4.5 copy-start.29
  62.7 4.7 copy-start.27
  62.8 5.0 copy-start.25
  62.8 5.2 copy-start.23
  62.8 5.5 copy-start.21
  62.8 5.7 copy-start.19
  62.8 5.9 copy-start.17
  62.8 6.1 copy-start.15
  62.8 6.4 copy-start.13
  62.8 6.6 copy-start.11
  62.8 6.8 copy-start.9
  62.8 7.0 copy-start.7
  62.9 7.3 copy-start.5
  62.9 7.5 copy-start.3
  62.9 7.7 copy-start.1
  74.2 896.5 %reduce-scatter.3.cloned.1.call-start = ((), (), s32[]{:S(2)}) async-start(), calls=%async_computation.2 | async-start | bytes 4423680 | tf_op jit(solution)/shard_map/reduce_scatter | solution.py:83
  152.7 6.0 copy-start.44
  152.7 6.2 copy-start.42
  152.7 6.4 copy-start.40
  152.7 6.7 copy-start.38
  152.7 6.9 copy-start.36
  153.9 6.0 copy-start.34
  155.1 5.0 copy-start.32
  156.3 4.1 copy-start.30
  (52 other events, 129.2 us)
Sparse Core Ops, SparseCore 0:
  74.4 819.2 all-reduce.3
  898.6 72.1 reduce-scatter.2
